TPU v7x, 32 devices: a whole 2x2x4 slice. The times are simulated.
32 devices in a mesh: hi: 4 (over z), mid: 4 (over x, core), lo: 2 (over y).
Axes of the slice: x: 2, y: 2, z: 4, core: 2. Of those that a mesh axis runs over, the one named last changes fastest.
Arguments:
- amplitudes: bfloat16 [1024, 16384], P('lo', ('hi', 'mid')), may hold values from -6 to 6
- hop_blocks: bfloat16 [4, 512, 512], replicated, may hold values from -1 to 2, as said below
- coupling_seed: int32 [14], replicated, may hold values from 1 to 7
Outputs:
- new_state: bfloat16 [1024, 16384], P('lo', ('hi', 'mid'))
Inputs may be any that keep to these rules, and one draw needn't show every extreme that they name: hop_blocks[k, a, b] is zero where a and b differ in their number of set bits.
All inputs are finite; a program needn't handle non-finite values.
Results may differ from a plain program's by a relative error of at most 0.0064.
Values may be sent and summed in bfloat16 or wider, within the bound.
A program may use at most 64 MiB of HBM per device.

v0:
```python
import jax
import jax.numpy as jnp
from jax import lax
from jax.sharding import PartitionSpec as P

BLOCK = 512
SITES = 14
COUPLING = 0.06


def occupancy(indices):
    site_ids = jnp.arange(SITES, dtype=jnp.int32)
    return (indices[:, None] >> site_ids[None, :] & 1).astype(jnp.float32)


def diagonal_factor(up_index, down_index, coupling_seed):
    up_occupied = occupancy(up_index)
    down_occupied = occupancy(down_index)
    strength = COUPLING * coupling_seed.astype(jnp.float32)
    energy = jnp.dot(
        up_occupied * strength[None, :], down_occupied.T, precision=lax.Precision.HIGHEST
    )
    return jnp.exp(-energy)


def on_device(amplitudes, hop_blocks, coupling_seed):
    down_rows, up_cols = amplitudes.shape
    groups = lax.axis_size(("hi", "mid"))
    lo_count = lax.axis_size("lo")
    split_view = amplitudes.reshape(down_rows, up_cols // BLOCK, BLOCK)
    first_pass = jnp.einsum(
        "dav,wv->awd", split_view, hop_blocks[0], preferred_element_type=jnp.float32
    ).astype(jnp.bfloat16)
    local_top = BLOCK // groups
    remainder = up_cols // local_top
    first_pass = first_pass.reshape(local_top, remainder, down_rows)
    moved = lax.all_to_all(first_pass, ("hi", "mid"), split_axis=1, concat_axis=0, tiled=True)
    second_pass = jnp.einsum(
        "gh,hpd->gpd", hop_blocks[1], moved, preferred_element_type=jnp.float32
    )
    span_low = remainder // groups
    up_index = (
        jnp.arange(BLOCK, dtype=jnp.int32)[:, None] * remainder
        + lax.axis_index(("hi", "mid")) * span_low
        + jnp.arange(span_low, dtype=jnp.int32)[None, :]
    ).reshape(-1)
    down_index = lax.axis_index("lo") * down_rows + jnp.arange(down_rows, dtype=jnp.int32)
    factor = diagonal_factor(up_index, down_index, coupling_seed).reshape(
        BLOCK, span_low, down_rows
    )
    mixed_pass = (second_pass * factor).astype(jnp.bfloat16)
    returned = lax.all_to_all(
        mixed_pass, ("hi", "mid"), split_axis=0, concat_axis=1, tiled=True
    ).reshape(up_cols, down_rows)
    third_pass = jnp.einsum(
        "ud,ed->eu", returned, hop_blocks[2], preferred_element_type=jnp.float32
    ).astype(jnp.bfloat16)
    gathered = lax.all_to_all(
        third_pass.reshape(BLOCK // lo_count, lo_count, up_cols),
        "lo",
        split_axis=1,
        concat_axis=0,
        tiled=True,
    )
    fourth_pass = jnp.einsum(
        "gh,hpu->gpu", hop_blocks[3], gathered, preferred_element_type=jnp.float32
    ).astype(jnp.bfloat16)
    result = lax.all_to_all(fourth_pass, "lo", split_axis=0, concat_axis=1, tiled=True).reshape(
        down_rows, up_cols
    )
    return result


def solution(mesh):
    in_specs = (P("lo", ("hi", "mid")), P(), P())
    out_specs = P("lo", ("hi", "mid"))
    return jax.shard_map(
        on_device, mesh=mesh, in_specs=in_specs, out_specs=out_specs, check_vma=False
    )
```

profile of v0, /device:TPU:0, one launch (start us, length us, event | category | flops | bytes accessed | tf_op | source)
XLA Modules:
  0.0 115.0 jit_solution(5764832066527705775)
XLA Ops:
  0.0 2.1 %convolution_convert_fusion.2 = bf16[512,512,2]{1,0,2:T(8,128)(2,1)S(1)} fusion(bf16[64,2,8,512]{3,2,1,0:T(8,128)(2,1)} %bitcast.57, bf16[4,512,512]{2,1,0:T(8,128)(2,1)} %param.4), kind=kOutput, calls=%fused_computation.5 | convolution fusion | flops 537395200 | bytes 2621440 | tf_op jit(solution)/shard_map/dav,wv->awd/dot_general | solution.py:31
  2.1 0.0 copy-start
  2.1 1.5 %copy.56 = bf16[32,32,512]{2,0,1:T(8,128)(2,1)} copy(bf16[32,32,512]{2,1,0:T(8,128)(2,1)S(1)} %bitcast.56) | data formatting | bytes 2097152 | tf_op jit(solution)/shard_map/reshape | solution.py:36
  3.7 7.4 %all-to-all-start = ((bf16[32,32,512]{2,0,1:T(8,128)(2,1)}), bf16[32,32,512]{2,0,1:T(8,128)(2,1)S(1)}, u32[]{:S(2)}, u32[]{:S(2)}) async-start(bf16[32,32,512]{2,0,1:T(8,128)(2,1)} %copy.56), calls=%async_computation | async-start | bytes 2097152 | tf_op jit(solution)/shard_map/all_to_all | solution.py:37
  11.1 0.1 iota_add_fusion
  11.2 0.2 add.50
  11.4 0.0 copy-done
  11.5 2.0 %negate_exponential_fusion = f32[1024,512]{1,0:T(8,128)S(1)} fusion(s32[512]{0:T(512)S(1)} %iota_add_fusion.1, f32[14]{0:T(128)S(1)} %convert_multiply_fusion, s32[1024]{0:T(1024)S(1)} %add.50), kind=kOutput, calls=%fused_computation.2 | convolution fusion | flops 88683520 | bytes 2103352 | tf_op jit(solution)/shard_map/dot_general | solution.py:20
  13.4 2.3 %reshape.54 = f32[512,2,512]{2,1,0:T(2,128)} reshape(f32[1024,512]{1,0:T(8,128)S(1)} %negate_exponential_fusion) | data formatting | bytes 4194304 | tf_op jit(solution)/shard_map/reshape | solution.py:48
  15.7 2.7 %copy.59 = f32[512,2,512]{0,2,1:T(8,128)S(1)} copy(f32[512,2,512]{2,1,0:T(2,128)} %reshape.54) | data formatting | bytes 4194304 | tf_op jit(solution)/shard_map/reshape | solution.py:48
  18.5 15.5 %all-to-all-done = bf16[32,32,512]{2,0,1:T(8,128)(2,1)S(1)} async-done(((bf16[32,32,512]{2,0,1:T(8,128)(2,1)}), bf16[32,32,512]{2,0,1:T(8,128)(2,1)S(1)}, u32[]{:S(2)}, u32[]{:S(2)}) %all-to-all-start) | async-done | bytes 1048608 | tf_op jit(solution)/shard_map/all_to_all | solution.py:37
  34.0 0.1 copy.57
  34.1 1.8 %fusion = bf16[512,2,512]{0,2,1:T(8,128)(2,1)S(1)} fusion(f32[512,2,512]{0,2,1:T(8,128)S(1)} %copy.59, bf16[512,2,512]{2,0,1:T(8,128)(2,1)S(1)} %bitcast.54, bf16[4,512,512]{2,1,0:T(8,128)(2,1)} %param.4), kind=kOutput, calls=%fused_computation.1 | convolution fusion | flops 537919488 | bytes 4718592 | tf_op jit(solution)/shard_map/gh,hpd->gpd/dot_general | solution.py:38
  35.9 1.0 copy.60
  36.9 31.3 %all_to_all.63 = bf16[512,2,512]{2,1,0:T(2,128)(2,1)S(1)} all-to-all(bf16[512,2,512]{2,1,0:T(2,128)(2,1)S(1)} %copy.60), channel_id=1, replica_groups=mesh['hi'=4,'mid'=4,'lo'=2] {'hi','mid'}, dimensions={0} | all-to-all | bytes 2097152 | tf_op jit(solution)/shard_map/all_to_all | solution.py:52
  68.1 0.2 copy.61
  68.3 1.1 copy.62
  69.4 0.4 reshape.55
  69.8 1.8 %fusion.1 = bf16[512,1024]{1,0:T(8,128)(2,1)S(1)} fusion(bf16[1024,512]{1,0:T(8,128)(2,1)S(1)} %reshape.55, bf16[4,512,512]{2,1,0:T(8,128)(2,1)} %param.4), kind=kOutput, calls=%fused_computation.6 | convolution fusion | flops 537395200 | bytes 2621440 | tf_op jit(solution)/shard_map/ud,ed->eu/dot_general | solution.py:55
  71.6 0.4 reshape.56
  72.1 0.3 copy.63
  72.4 17.5 %all_to_all.64 = bf16[256,2,1024]{2,0,1:T(8,128)(2,1)S(1)} all-to-all(bf16[256,2,1024]{2,0,1:T(8,128)(2,1)S(1)} %copy.63), channel_id=1, replica_groups=mesh['hi'=4,'mid'=4,'lo'=2] {'lo'}, dimensions={1} | all-to-all | bytes 2097152 | tf_op jit(solution)/shard_map/all_to_all | solution.py:58
  89.8 1.8 %fusion.2 = bf16[512,1,1024]{0,2,1:T(8,128)(2,1)S(1)} fusion(bf16[512,1024]{1,0:T(8,128)(2,1)S(1)} %bitcast.55, bf16[4,512,512]{2,1,0:T(8,128)(2,1)} %param.4), kind=kOutput, calls=%fused_computation.7 | convolution fusion | flops 537395200 | bytes 2621440 | tf_op jit(solution)/shard_map/gh,hpu->gpu/dot_general | solution.py:65
  91.6 0.5 broadcast.24
  92.1 1.5 %reduce = bf16[512,1024]{0,1:T(8,128)(2,1)S(1)} reduce(bf16[512,1,1024]{0,2,1:T(8,128)(2,1)S(1)} %fusion.2, bf16[]{:T(256)} %broadcast.24), dimensions={1}, to_apply=%copy.64.reduce_sub_computation | reduce | bytes 2097154 | tf_op jit(solution)/shard_map/convert_element_type | solution.py:67
  93.6 0.5 copy.73
  94.1 0.8 reshape.61
  94.9 16.5 %all_to_all.65 = bf16[2,2,131072]{2,1,0:T(2,128)(2,1)S(1)} all-to-all(bf16[2,2,131072]{2,1,0:T(2,128)(2,1)S(1)} %reshape.61), channel_id=1, replica_groups=mesh['hi'=4,'mid'=4,'lo'=2] {'lo'}, dimensions={0} | all-to-all | bytes 2097152 | tf_op jit(solution)/shard_map/all_to_all | solution.py:68
  111.4 0.9 reshape.62
  112.3 0.4 copy.67
  112.7 1.1 copy.65
  113.8 1.2 %reshape.58 = bf16[512,1024]{1,0:T(8,128)(2,1)} reshape(bf16[256,2,1,1024]{3,1,0,2:T(2,128)(2,1)S(1)} %copy.65) | data formatting | bytes 2097152 | tf_op jit(solution)/shard_map/reshape | solution.py:68
  (3 shorter events, 0.0 us)
Async XLA Ops:
  2.1 9.3 %copy-start = (s32[14]{0:T(128)S(1)}, s32[14]{0:T(128)}, u32[]{:S(2)}) copy-start(s32[14]{0:T(128)} %param.5) | copy-start | bytes 172
  3.7 30.3 %all-to-all-start = ((bf16[32,32,512]{2,0,1:T(8,128)(2,1)}), bf16[32,32,512]{2,0,1:T(8,128)(2,1)S(1)}, u32[]{:S(2)}, u32[]{:S(2)}) async-start(bf16[32,32,512]{2,0,1:T(8,128)(2,1)} %copy.56), calls=%async_computation | async-start | bytes 2097152 | tf_op jit(solution)/shard_map/all_to_all | solution.py:37
where the time goes:
time: 116 us; the launch traced here: 115 us
  blocking collectives  65.2 us (56%)
  local copies, waits for them, and re-layouts  15.7 us (14%)
  waiting for transfers between devices  15.5 us (13%)
  matrix products  9.51 us (8%)
  starting transfers between devices  7.39 us (6%)
  other arithmetic  1.59 us (1%)
    all_to_all x1, blocking collectives, on_device(): lax.all_to_all(mixed_pass, ('hi', 'mid'), split_axis=0, concat_axis=1, ti...  31.3 us
    all_to_all x1, blocking collectives, on_device(): lax.all_to_all(third_pass.reshape(BLOCK // lo_count, lo_count, up_cols),...  17.5 us
    all_to_all x1, blocking collectives, on_device(): lax.all_to_all(fourth_pass, 'lo', split_axis=0, concat_axis=1, tiled=True)  16.5 us
    all_to_all x1, waiting for transfers between devices, on_device(): lax.all_to_all(first_pass, ('hi', 'mid'), split_axis=1, concat_axis=0, ti...  15.5 us
    all_to_all x1, starting transfers between devices, on_device(): lax.all_to_all(first_pass, ('hi', 'mid'), split_axis=1, concat_axis=0, ti...  7.39 us
    reshape x2, local copies, waits for them, and re-layouts, on_device(): diagonal_factor(up_index, down_index, coupling_seed)  5.05 us
    unnamed x6, local copies, waits for them, and re-layouts  2.63 us
  transfers between devices with their start and end apart: 1, of which 1 were waited for; matrix products, arithmetic and copies ran while one was open for 6% of the time, Pallas kernels for 0%

commit v1 on v0

--- a/solution.py
+++ b/solution.py
@@ -65,9 +65,10 @@
     fourth_pass = jnp.einsum(
         "gh,hpu->gpu", hop_blocks[3], gathered, preferred_element_type=jnp.float32
     ).astype(jnp.bfloat16)
-    result = lax.all_to_all(fourth_pass, "lo", split_axis=0, concat_axis=1, tiled=True).reshape(
-        down_rows, up_cols
-    )
+    result = jnp.concatenate(
+        lax.all_to_all(jnp.stack(jnp.split(fourth_pass, lax.axis_size("lo"), axis=0)), "lo", 0, 0),
+        axis=1,
+    ).reshape(down_rows, up_cols)
     return result
 
 

time: 116 us -> 111 us (0.957)
  local copies, waits for them, and re-layouts: 15.7 us -> 12.6 us
  other arithmetic: 1.59 us -> 0.24 us
    unnamed x6 -> x2, local copies, waits for them, and re-layouts: 2.63 us -> 0.01 us
    convert_element_type x1 -> x0, other arithmetic: 1.45 us -> none  [on_device(): fourth_pass = jnp.einsum('gh,hpu->gpu', hop_blocks[3], gathered, preferre...]
    another operation x0 -> x2, local copies, waits for them, and re-layouts: none -> 1.29 us  [the longest x1 1.22 us: on_device(): result = jnp.concatenate(lax.all_to_all(jnp.stack(jnp.split(fourth_pass,...]
  transfers between devices with their start and end apart: 1 -> 1, of which waited for: 1 -> 1; matrix products, arithmetic and copies ran while one was open for 6% -> 7% of each run, Pallas kernels for 0% -> 0%
where the time goes in v1:
time: 111 us
  blocking collectives  65.2 us (59%)
  waiting for transfers between devices  15.5 us (14%)
  local copies, waits for them, and re-layouts  12.6 us (11%)
  matrix products  9.51 us (9%)
  starting transfers between devices  7.39 us (7%)
    all_to_all x1, blocking collectives, on_device(): lax.all_to_all(mixed_pass, ('hi', 'mid'), split_axis=0, concat_axis=1, ti...  31.3 us
    all_to_all x1, blocking collectives, on_device(): lax.all_to_all(third_pass.reshape(BLOCK // lo_count, lo_count, up_cols),...  17.5 us
    all_to_all x1, blocking collectives, on_device(): lax.all_to_all(jnp.stack(jnp.split(fourth_pass, lax.axis_size('lo'), axis...  16.5 us
    all_to_all x1, waiting for transfers between devices, on_device(): lax.all_to_all(first_pass, ('hi', 'mid'), split_axis=1, concat_axis=0, ti...  15.5 us
    all_to_all x1, starting transfers between devices, on_device(): lax.all_to_all(first_pass, ('hi', 'mid'), split_axis=1, concat_axis=0, ti...  7.39 us
    reshape x2, local copies, waits for them, and re-layouts, on_device(): diagonal_factor(up_index, down_index, coupling_seed)  5.03 us
  transfers between devices with their start and end apart: 1, of which 1 were waited for; matrix products, arithmetic and copies ran while one was open for 7% of the time, Pallas kernels for 0%

profile of v1, /device:TPU:0, one launch (start us, length us, event | category | flops | bytes accessed | tf_op | source)
XLA Modules:
  0.0 110.6 jit_solution(7790981644420754204)
XLA Ops:
  0.0 2.1 %convolution_convert_fusion.2 = bf16[512,512,2]{1,0,2:T(8,128)(2,1)S(1)} fusion(bf16[64,2,8,512]{3,2,1,0:T(8,128)(2,1)} %bitcast.57, bf16[4,512,512]{2,1,0:T(8,128)(2,1)} %param.4), kind=kOutput, calls=%fused_computation.5 | convolution fusion | flops 537395200 | bytes 2621440 | tf_op jit(solution)/shard_map/dav,wv->awd/dot_general | solution.py:31
  2.1 0.0 copy-start
  2.1 1.5 %copy.33 = bf16[32,32,512]{2,0,1:T(8,128)(2,1)} copy(bf16[32,32,512]{2,1,0:T(8,128)(2,1)S(1)} %bitcast.56) | data formatting | bytes 2097152 | tf_op jit(solution)/shard_map/reshape | solution.py:36
  3.7 7.4 %all-to-all-start = ((bf16[32,32,512]{2,0,1:T(8,128)(2,1)}), bf16[32,32,512]{2,0,1:T(8,128)(2,1)S(1)}, u32[]{:S(2)}, u32[]{:S(2)}) async-start(bf16[32,32,512]{2,0,1:T(8,128)(2,1)} %copy.33), calls=%async_computation | async-start | bytes 2097152 | tf_op jit(solution)/shard_map/all_to_all | solution.py:37
  11.1 0.1 iota_add_fusion
  11.2 0.2 add.50
  11.4 0.0 copy-done
  11.5 2.0 %negate_exponential_fusion = f32[1024,512]{1,0:T(8,128)S(1)} fusion(s32[512]{0:T(512)S(1)} %iota_add_fusion.1, f32[14]{0:T(128)S(1)} %convert_multiply_fusion, s32[1024]{0:T(1024)S(1)} %add.50), kind=kOutput, calls=%fused_computation.2 | convolution fusion | flops 88683520 | bytes 2103352 | tf_op jit(solution)/shard_map/dot_general | solution.py:20
  13.4 2.3 %reshape.57 = f32[512,2,512]{2,1,0:T(2,128)} reshape(f32[1024,512]{1,0:T(8,128)S(1)} %negate_exponential_fusion) | data formatting | bytes 4194304 | tf_op jit(solution)/shard_map/reshape | solution.py:48
  15.7 2.7 %copy.36 = f32[512,2,512]{0,2,1:T(8,128)S(1)} copy(f32[512,2,512]{2,1,0:T(2,128)} %reshape.57) | data formatting | bytes 4194304 | tf_op jit(solution)/shard_map/reshape | solution.py:48
  18.5 15.5 %all-to-all-done = bf16[32,32,512]{2,0,1:T(8,128)(2,1)S(1)} async-done(((bf16[32,32,512]{2,0,1:T(8,128)(2,1)}), bf16[32,32,512]{2,0,1:T(8,128)(2,1)S(1)}, u32[]{:S(2)}, u32[]{:S(2)}) %all-to-all-start) | async-done | bytes 1048608 | tf_op jit(solution)/shard_map/all_to_all | solution.py:37
  34.0 0.1 copy.34
  34.1 1.8 %fusion = bf16[512,2,512]{0,2,1:T(8,128)(2,1)S(1)} fusion(f32[512,2,512]{0,2,1:T(8,128)S(1)} %copy.36, bf16[512,2,512]{2,0,1:T(8,128)(2,1)S(1)} %bitcast.54, bf16[4,512,512]{2,1,0:T(8,128)(2,1)} %param.4), kind=kOutput, calls=%fused_computation.1 | convolution fusion | flops 537919488 | bytes 4718592 | tf_op jit(solution)/shard_map/gh,hpd->gpd/dot_general | solution.py:38
  35.9 1.0 copy.37
  36.9 31.3 %all_to_all.53 = bf16[512,2,512]{2,1,0:T(2,128)(2,1)S(1)} all-to-all(bf16[512,2,512]{2,1,0:T(2,128)(2,1)S(1)} %copy.37), channel_id=1, replica_groups=mesh['hi'=4,'mid'=4,'lo'=2] {'hi','mid'}, dimensions={0} | all-to-all | bytes 2097152 | tf_op jit(solution)/shard_map/all_to_all | solution.py:52
  68.1 0.2 copy.38
  68.3 1.1 copy.39
  69.4 0.4 reshape.58
  69.8 1.8 %fusion.1 = bf16[512,1024]{1,0:T(8,128)(2,1)S(1)} fusion(bf16[1024,512]{1,0:T(8,128)(2,1)S(1)} %reshape.58, bf16[4,512,512]{2,1,0:T(8,128)(2,1)} %param.4), kind=kOutput, calls=%fused_computation.6 | convolution fusion | flops 537395200 | bytes 2621440 | tf_op jit(solution)/shard_map/ud,ed->eu/dot_general | solution.py:55
  71.6 0.4 reshape.59
  72.1 0.3 copy.40
  72.4 17.5 %all_to_all.54 = bf16[256,2,1024]{2,0,1:T(8,128)(2,1)S(1)} all-to-all(bf16[256,2,1024]{2,0,1:T(8,128)(2,1)S(1)} %copy.40), channel_id=1, replica_groups=mesh['hi'=4,'mid'=4,'lo'=2] {'lo'}, dimensions={1} | all-to-all | bytes 2097152 | tf_op jit(solution)/shard_map/all_to_all | solution.py:58
  89.8 1.8 %fusion.2 = bf16[512,1024]{0,1:T(8,128)(2,1)S(1)} fusion(bf16[512,1024]{1,0:T(8,128)(2,1)S(1)} %bitcast.55, bf16[4,512,512]{2,1,0:T(8,128)(2,1)} %param.4), kind=kOutput, calls=%fused_computation.7 | convolution fusion | flops 537395200 | bytes 2621440 | tf_op jit(solution)/shard_map/gh,hpu->gpu/dot_general | solution.py:65
  91.6 0.1 slice_bitcast_fusion.1
  91.7 0.1 pad_maximum_fusion
  91.8 16.5 %all_to_all.55 = bf16[2,256,1,1024]{1,3,2,0:T(8,128)(2,1)S(1)} all-to-all(bf16[2,256,1,1024]{1,3,2,0:T(8,128)(2,1)S(1)} %pad_maximum_fusion), channel_id=1, replica_groups=mesh['hi'=4,'mid'=4,'lo'=2] {'lo'}, dimensions={0} | all-to-all | bytes 2097152 | tf_op jit(solution)/shard_map/all_to_all | solution.py:69
  108.3 1.1 copy.41
  109.4 1.2 %reshape_reshape.3 = bf16[512,1024]{1,0:T(8,128)(2,1)} reshape(bf16[256,2,1,1024]{3,1,0,2:T(2,128)(2,1)S(1)} %copy.41) | data formatting | bytes 2097152 | tf_op jit(solution)/shard_map/reshape;reshape | solution.py:71
  (3 shorter events, 0.0 us)
Async XLA Ops:
  2.1 9.3 %copy-start = (s32[14]{0:T(128)S(1)}, s32[14]{0:T(128)}, u32[]{:S(2)}) copy-start(s32[14]{0:T(128)} %param.5) | copy-start | bytes 172
  3.7 30.3 %all-to-all-start = ((bf16[32,32,512]{2,0,1:T(8,128)(2,1)}), bf16[32,32,512]{2,0,1:T(8,128)(2,1)S(1)}, u32[]{:S(2)}, u32[]{:S(2)}) async-start(bf16[32,32,512]{2,0,1:T(8,128)(2,1)} %copy.33), calls=%async_computation | async-start | bytes 2097152 | tf_op jit(solution)/shard_map/all_to_all | solution.py:37
